TPU v7x, 32 devices: a whole 2x2x4 slice. The times are simulated.
32 devices in a mesh: replica: 2 (over y), fsdp: 8 (over z, core), seq: 2 (over x).
Axes of the slice: x: 2, y: 2, z: 4, core: 2. Of those that a mesh axis runs over, the one named last changes fastest.
Arguments:
- series_in: bfloat16 [16, 512, 1280], P(('replica', 'fsdp'), 'seq'), may hold values from -6 to 6
- cotangent: bfloat16 [16, 512, 1280], P(('replica', 'fsdp'), 'seq'), may hold values from -6 to 6
- qkv_weight: bfloat16 [2, 1280, 3840], P(None, 'fsdp'), may hold values from -0.15625 to 0.15625
- out_weight: bfloat16 [2, 1280, 1280], P(None, 'fsdp'), may hold values from -0.625 to 0.625
- up_weight: bfloat16 [2, 1280, 1280], P(None, 'fsdp'), may hold values from -0.15625 to 0.15625
- down_weight: bfloat16 [2, 1280, 1280], P(None, 'fsdp'), may hold values from -0.15625 to 0.15625
- norm_gains: bfloat16 [2, 2, 1280], P(None, None, 'fsdp'), may hold values from 0.25 to 1.75
- up_bias: bfloat16 [2, 1280], P(None, 'fsdp'), may hold values from -3 to 3
- down_bias: bfloat16 [2, 1280], P(None, 'fsdp'), may hold values from -2 to 2
- query_scale: bfloat16 [2, 80], P(None, 'fsdp'), may hold values from -1 to 1
- pad_length: int32 [16], P(('replica', 'fsdp')), may hold values from 0 to 128, as said below
- span_starts: int32 [16, 4], P(('replica', 'fsdp')), may hold values from 0 to 480, as said below
- span_count: int32 [16], P(('replica', 'fsdp')), may hold values from 1 to 4, as said below
Outputs:
- series_out: bfloat16 [16, 512, 1280], P(('replica', 'fsdp'), 'seq')
- input_grad: bfloat16 [16, 512, 1280], P(('replica', 'fsdp'), 'seq')
- grad_qkv: float32 [2, 1280, 3840], P(None, 'fsdp')
- grad_out: float32 [2, 1280, 1280], P(None, 'fsdp')
- grad_up: float32 [2, 1280, 1280], P(None, 'fsdp')
- grad_down: float32 [2, 1280, 1280], P(None, 'fsdp')
- grad_gains: float32 [2, 2, 1280], P(None, None, 'fsdp')
- grad_up_bias: float32 [2, 1280], P(None, 'fsdp')
- grad_down_bias: float32 [2, 1280], P(None, 'fsdp')
- grad_query_scale: float32 [2, 80], P(None, 'fsdp')
Inputs may be any that keep to these rules, and one draw needn't show every extreme that they name: `pad_length`: one series in every draw has exactly 128 padded positions. `span_starts`: slot 0 of every series starts within 31 positions before 256, so it holds positions 255 and 256; spans may intersect. Slot k of series b is used when k < span_count[b].
All inputs are finite; a program needn't handle non-finite values.
Results may differ from a plain program's by a relative error of at most 0.025.
Values may be sent and summed in bfloat16 or wider, within the bound.
A program may use at most 256 MiB of HBM per device.

v0:
```python
import math
import jax
import jax.numpy as jnp
from jax import lax
from jax.sharding import PartitionSpec as P

HEADS = 16
HEAD = 80
SPAN = 32
EPSILON = 1e-06
SOFT_ONE = 1.442695041
NEG_FILL = -1e30


def visible(pad_length, span_starts, span_count, offset, local_length, total_length):
    query_pos = offset + jnp.arange(local_length, dtype=jnp.int32)
    key_pos = jnp.arange(total_length, dtype=jnp.int32)
    shared = jnp.zeros((span_starts.shape[0], local_length, total_length), dtype=bool)
    for slot_index in range(span_starts.shape[1]):
        slot_start = span_starts[:, slot_index]
        slot_used = slot_index < span_count
        query_in = (
            slot_used[:, None]
            & (query_pos[None, :] >= slot_start[:, None])
            & (query_pos[None, :] < slot_start[:, None] + SPAN)
        )
        key_in = (key_pos[None, :] >= slot_start[:, None]) & (
            key_pos[None, :] < slot_start[:, None] + SPAN
        )
        shared = shared | query_in[:, :, None] & key_in[:, None, :]
    causal = key_pos[None, :] <= query_pos[:, None]
    allowed = (key_pos[None, None, :] >= pad_length[:, None, None]) & (causal[None] | shared)
    return allowed | (key_pos[None, None, :] == query_pos[None, :, None])


def norm_rows(values, scale_gain):
    inverse = lax.rsqrt(jnp.mean(values * values, axis=-1, keepdims=True) + EPSILON)
    return (values * inverse * scale_gain, inverse)


def norm_back(values, inverse, scale_gain, upstream):
    scaled = upstream * scale_gain
    inner_term = jnp.mean(values * scaled, axis=-1, keepdims=True)
    result = inverse * scaled - values * (inverse * inverse * inverse) * inner_term
    return (result, jnp.sum(upstream * values * inverse, axis=0))


def query_factor(query_scale):
    return jax.nn.softplus(query_scale.astype(jnp.float32)) * (SOFT_ONE / math.sqrt(HEAD))


def forward_layer(current, weights, allowed, series_count, local_length, total_length):
    qkv_weight, out_weight, up_weight, down_weight, norm_gains, up_bias, down_bias, query_scale = (
        weights
    )
    token_count, model_width = current.shape
    normed, inverse_one = norm_rows(current, norm_gains[0].astype(jnp.float32))
    normed_low = normed.astype(jnp.bfloat16).reshape(series_count, local_length, model_width)
    projected = jnp.einsum(
        "bld,dc->bcl", normed_low, qkv_weight, preferred_element_type=jnp.float32
    )
    query_raw = projected[:, :model_width]
    factor = query_factor(query_scale)
    query_low = (
        query_raw.reshape(series_count, HEADS, HEAD, local_length) * factor[None, None, :, None]
    ).astype(jnp.bfloat16)
    pair_low = projected[:, model_width:].astype(jnp.bfloat16)
    pair_all = lax.all_gather(pair_low, "seq", axis=2, tiled=True)
    key_all = pair_all[:, :model_width].reshape(series_count, HEADS, HEAD, total_length)
    value_all = pair_all[:, model_width:].reshape(series_count, HEADS, HEAD, total_length)
    scores = jnp.einsum("bheq,bhek->bhqk", query_low, key_all, preferred_element_type=jnp.float32)
    scores = jnp.where(allowed[:, None], scores, NEG_FILL)
    top_score = jnp.max(scores, axis=-1, keepdims=True)
    exp_scores = jnp.exp(scores - top_score)
    exp_total = jnp.sum(exp_scores, axis=-1, keepdims=True)
    probs_low = (exp_scores / exp_total).astype(jnp.bfloat16)
    log_total = top_score + jnp.log(exp_total)
    attended = jnp.einsum(
        "bhqk,bhek->bheq", probs_low, value_all, preferred_element_type=jnp.float32
    )
    attended_low = attended.astype(jnp.bfloat16).reshape(series_count, model_width, local_length)
    attn_out = jnp.einsum(
        "bdl,de->ble", attended_low, out_weight, preferred_element_type=jnp.float32
    )
    after_attn = current + attn_out.reshape(token_count, model_width)
    normed_two, inverse_two = norm_rows(after_attn, norm_gains[1].astype(jnp.float32))
    mixed_low = normed_two.astype(jnp.bfloat16)
    hidden_pre = jnp.dot(mixed_low, up_weight, preferred_element_type=jnp.float32) + up_bias.astype(
        jnp.float32
    )
    hidden_low = jax.nn.silu(hidden_pre).astype(jnp.bfloat16)
    result = after_attn + (
        jnp.dot(hidden_low, down_weight, preferred_element_type=jnp.float32)
        + down_bias.astype(jnp.float32)
    )
    stored = (
        current,
        inverse_one,
        normed_low,
        query_raw,
        query_low,
        key_all,
        value_all,
        log_total,
        attended_low,
        after_attn,
        inverse_two,
        mixed_low,
        hidden_pre,
        hidden_low,
    )
    return (result, stored)


def backward_layer(upstream, weights, stored, allowed, series_count, local_length, total_length):
    qkv_weight, out_weight, up_weight, down_weight, norm_gains, up_bias, down_bias, query_scale = (
        weights
    )
    (
        current,
        inverse_one,
        normed_low,
        query_raw,
        query_low,
        key_all,
        value_all,
        log_total,
        attended_low,
        after_attn,
        inverse_two,
        mixed_low,
        hidden_pre,
        hidden_low,
    ) = stored
    token_count, model_width = current.shape
    down_low = upstream.astype(jnp.bfloat16)
    grad_down_bias = jnp.sum(down_low, axis=0, dtype=jnp.float32)
    grad_down = jnp.einsum("tf,td->fd", hidden_low, down_low, preferred_element_type=jnp.float32)
    hidden_grad = jnp.einsum("td,fd->tf", down_low, down_weight, preferred_element_type=jnp.float32)
    sigmoid_pre = jax.nn.sigmoid(hidden_pre)
    pre_low = (hidden_grad * sigmoid_pre * (1.0 + hidden_pre * (1.0 - sigmoid_pre))).astype(
        jnp.bfloat16
    )
    grad_up_bias = jnp.sum(pre_low, axis=0, dtype=jnp.float32)
    grad_up = jnp.einsum("td,tf->df", mixed_low, pre_low, preferred_element_type=jnp.float32)
    mixed_grad = jnp.einsum("tf,df->td", pre_low, up_weight, preferred_element_type=jnp.float32)
    norm_grad_two, gain_grad_two = norm_back(
        after_attn, inverse_two, norm_gains[1].astype(jnp.float32), mixed_grad
    )
    attn_grad = upstream + norm_grad_two
    branch_low = attn_grad.astype(jnp.bfloat16).reshape(series_count, local_length, model_width)
    grad_out = jnp.einsum(
        "bdl,ble->de", attended_low, branch_low, preferred_element_type=jnp.float32
    )
    output_low = (
        jnp.einsum("ble,de->bdl", branch_low, out_weight, preferred_element_type=jnp.float32)
        .astype(jnp.bfloat16)
        .reshape(series_count, HEADS, HEAD, local_length)
    )
    scores = jnp.einsum("bheq,bhek->bhqk", query_low, key_all, preferred_element_type=jnp.float32)
    scores = jnp.where(allowed[:, None], scores, NEG_FILL)
    attn_probs = jnp.exp(scores - log_total)
    prob_grad = jnp.einsum(
        "bheq,bhek->bhqk", output_low, value_all, preferred_element_type=jnp.float32
    )
    row_inner = jnp.sum(attn_probs * prob_grad, axis=-1, keepdims=True)
    score_low = (attn_probs * (prob_grad - row_inner)).astype(jnp.bfloat16)
    value_grad = jnp.einsum(
        "bhqk,bheq->bhek",
        attn_probs.astype(jnp.bfloat16),
        output_low,
        preferred_element_type=jnp.float32,
    )
    key_grad = jnp.einsum(
        "bhqk,bheq->bhek", score_low, query_low, preferred_element_type=jnp.float32
    )
    query_grad = jnp.einsum(
        "bhqk,bhek->bheq", score_low, key_all, preferred_element_type=jnp.float32
    )
    key_local, value_local = (
        lax.psum_scatter(
            key_grad.reshape(series_count, model_width, total_length),
            "seq",
            scatter_dimension=2,
            tiled=True,
        ),
        lax.psum_scatter(
            value_grad.reshape(series_count, model_width, total_length),
            "seq",
            scatter_dimension=2,
            tiled=True,
        ),
    )
    factor = query_factor(query_scale)
    factor_grad = jnp.sum(
        query_grad * query_raw.reshape(series_count, HEADS, HEAD, local_length), axis=(0, 1, 3)
    )
    grad_scale = (
        factor_grad * jax.nn.sigmoid(query_scale.astype(jnp.float32)) * (SOFT_ONE / math.sqrt(HEAD))
    )
    raw_low = (
        (query_grad * factor[None, None, :, None])
        .astype(jnp.bfloat16)
        .reshape(series_count, model_width, local_length)
    )
    projected_grad = jnp.concatenate(
        [raw_low, key_local.astype(jnp.bfloat16), value_local.astype(jnp.bfloat16)], axis=1
    )
    grad_qkv = jnp.einsum(
        "bld,bcl->dc", normed_low, projected_grad, preferred_element_type=jnp.float32
    )
    normed_grad = jnp.einsum(
        "bcl,dc->bld", projected_grad, qkv_weight, preferred_element_type=jnp.float32
    ).reshape(token_count, model_width)
    norm_grad_one, gain_grad_one = norm_back(
        current, inverse_one, norm_gains[0].astype(jnp.float32), normed_grad
    )
    result = attn_grad + norm_grad_one
    layer_grads = (
        grad_qkv,
        grad_out,
        grad_up,
        grad_down,
        jnp.stack([gain_grad_one, gain_grad_two]),
        grad_up_bias,
        grad_down_bias,
        grad_scale,
    )
    return (result, layer_grads)


def shards(
    series_in,
    cotangent,
    qkv_weight,
    out_weight,
    up_weight,
    down_weight,
    norm_gains,
    up_bias,
    down_bias,
    query_scale,
    pad_length,
    span_starts,
    span_count,
):
    series_count, local_length, model_width = series_in.shape
    seq_count = lax.axis_size("seq")
    total_length = local_length * seq_count
    offset = lax.axis_index("seq") * local_length
    allowed = visible(pad_length, span_starts, span_count, offset, local_length, total_length)
    layer_count = qkv_weight.shape[0]
    current = series_in.reshape(series_count * local_length, model_width).astype(jnp.float32)
    gathered_list = []
    stored_list = []
    for layer_index in range(layer_count):
        gathered = (
            lax.all_gather(qkv_weight[layer_index], "fsdp", axis=0, tiled=True),
            lax.all_gather(out_weight[layer_index], "fsdp", axis=0, tiled=True),
            lax.all_gather(up_weight[layer_index], "fsdp", axis=0, tiled=True),
            lax.all_gather(down_weight[layer_index], "fsdp", axis=0, tiled=True),
            lax.all_gather(norm_gains[layer_index], "fsdp", axis=1, tiled=True),
            lax.all_gather(up_bias[layer_index], "fsdp", axis=0, tiled=True),
            lax.all_gather(down_bias[layer_index], "fsdp", axis=0, tiled=True),
            lax.all_gather(query_scale[layer_index], "fsdp", axis=0, tiled=True),
        )
        current, stored = forward_layer(
            current, gathered, allowed, series_count, local_length, total_length
        )
        gathered_list.append(gathered)
        stored_list.append(stored)
    series_out = current.reshape(series_count, local_length, model_width).astype(jnp.bfloat16)
    upstream = cotangent.reshape(series_count * local_length, model_width).astype(jnp.float32)
    owned_list = [None] * layer_count
    for layer_index in reversed(range(layer_count)):
        gathered = (
            lax.all_gather(qkv_weight[layer_index], "fsdp", axis=0, tiled=True),
            lax.all_gather(out_weight[layer_index], "fsdp", axis=0, tiled=True),
            lax.all_gather(up_weight[layer_index], "fsdp", axis=0, tiled=True),
            lax.all_gather(down_weight[layer_index], "fsdp", axis=0, tiled=True),
            lax.all_gather(norm_gains[layer_index], "fsdp", axis=1, tiled=True),
            lax.all_gather(up_bias[layer_index], "fsdp", axis=0, tiled=True),
            lax.all_gather(down_bias[layer_index], "fsdp", axis=0, tiled=True),
            lax.all_gather(query_scale[layer_index], "fsdp", axis=0, tiled=True),
        )
        upstream, layer_grads = backward_layer(
            upstream,
            gathered,
            stored_list[layer_index],
            allowed,
            series_count,
            local_length,
            total_length,
        )
        shares = (
            lax.psum_scatter(
                layer_grads[0].astype(jnp.bfloat16), "fsdp", scatter_dimension=0, tiled=True
            ).astype(jnp.float32),
            lax.psum_scatter(
                layer_grads[1].astype(jnp.bfloat16), "fsdp", scatter_dimension=0, tiled=True
            ).astype(jnp.float32),
            lax.psum_scatter(
                layer_grads[2].astype(jnp.bfloat16), "fsdp", scatter_dimension=0, tiled=True
            ).astype(jnp.float32),
            lax.psum_scatter(
                layer_grads[3].astype(jnp.bfloat16), "fsdp", scatter_dimension=0, tiled=True
            ).astype(jnp.float32),
            lax.psum_scatter(
                layer_grads[4].astype(jnp.bfloat16), "fsdp", scatter_dimension=1, tiled=True
            ).astype(jnp.float32),
            lax.psum_scatter(
                layer_grads[5].astype(jnp.bfloat16), "fsdp", scatter_dimension=0, tiled=True
            ).astype(jnp.float32),
            lax.psum_scatter(
                layer_grads[6].astype(jnp.bfloat16), "fsdp", scatter_dimension=0, tiled=True
            ).astype(jnp.float32),
            lax.psum_scatter(
                layer_grads[7].astype(jnp.bfloat16), "fsdp", scatter_dimension=0, tiled=True
            ).astype(jnp.float32),
        )
        shares = (
            lax.psum(shares[0].astype(jnp.bfloat16), ("replica", "seq")).astype(jnp.float32),
            lax.psum(shares[1].astype(jnp.bfloat16), ("replica", "seq")).astype(jnp.float32),
            lax.psum(shares[2].astype(jnp.bfloat16), ("replica", "seq")).astype(jnp.float32),
            lax.psum(shares[3].astype(jnp.bfloat16), ("replica", "seq")).astype(jnp.float32),
            lax.psum(shares[4].astype(jnp.bfloat16), ("replica", "seq")).astype(jnp.float32),
            lax.psum(shares[5].astype(jnp.bfloat16), ("replica", "seq")).astype(jnp.float32),
            lax.psum(shares[6].astype(jnp.bfloat16), ("replica", "seq")).astype(jnp.float32),
            lax.psum(shares[7].astype(jnp.bfloat16), ("replica", "seq")).astype(jnp.float32),
        )
        owned_list[layer_index] = shares
    stacked = [
        jnp.stack([owned_list[layer_index][member_index] for layer_index in range(layer_count)])
        for member_index in range(8)
    ]
    input_grad = upstream.reshape(series_count, local_length, model_width).astype(jnp.bfloat16)
    return (
        series_out,
        input_grad,
        stacked[0],
        stacked[1],
        stacked[2],
        stacked[3],
        stacked[4],
        stacked[5],
        stacked[6],
        stacked[7],
    )


def solution(mesh):
    return jax.shard_map(
        shards,
        mesh=mesh,
        in_specs=(
            P(("replica", "fsdp"), "seq", None),
            P(("replica", "fsdp"), "seq", None),
            P(None, "fsdp", None),
            P(None, "fsdp", None),
            P(None, "fsdp", None),
            P(None, "fsdp", None),
            P(None, None, "fsdp"),
            P(None, "fsdp"),
            P(None, "fsdp"),
            P(None, "fsdp"),
            P(("replica", "fsdp")),
            P(("replica", "fsdp"), None),
            P(("replica", "fsdp")),
        ),
        out_specs=(
            P(("replica", "fsdp"), "seq", None),
            P(("replica", "fsdp"), "seq", None),
            P(None, "fsdp", None),
            P(None, "fsdp", None),
            P(None, "fsdp", None),
            P(None, "fsdp", None),
            P(None, None, "fsdp"),
            P(None, "fsdp"),
            P(None, "fsdp"),
            P(None, "fsdp"),
        ),
        check_vma=False,
    )
```

profile of v0, /device:TPU:0, one launch (start us, length us, event | category | flops | bytes accessed | tf_op | source)
XLA Modules:
  0.0 1406.5 jit_solution(13420251808383852536)
XLA Ops:
  10.7 17.4 %all-gather = bf16[1,2,1280]{1,0,2:T(2,128)(2,1)S(1)} all-gather(bf16[1,2,160]{1,0,2:T(2,128)(2,1)S(1)} %copy.71), channel_id=2, replica_groups=mesh['replica'=2,'fsdp'=8,'seq'=2] {'fsdp'}, dimensions={2}, use_global_device_ids=true | all-gather | bytes 5760 | tf_op jit(solution)/shard_map/all_gather | solution.py:262
  28.9 20.9 %fusion.139 = (f32[1280]{0:T(1024)S(1)}, f32[1280]{0:T(1024)S(1)}) fusion(bf16[1,2,1280]{1,0,2:T(2,128)(2,1)S(1)} %all-gather), kind=kLoop, calls=%fused_computation.149 | loop fusion | flops 2560 | bytes 15360 | tf_op jit(solution)/shard_map/mul | solution.py:38
  49.9 58.0 %all-gather.31.cloned.1.call-done = bf16[1,1280,3840]{2,1,0:T(8,128)(2,1)} async-done(((bf16[1,160,3840]{2,1,0:T(8,128)(2,1)}), bf16[1,1280,3840]{2,1,0:T(8,128)(2,1)}) %all-gather.31.cloned.1.call-update) | async-done | bytes 9830416 | tf_op jit(solution)/shard_map/all_gather | solution.py:258
  131.1 26.5 %all-reduce.13 = (bf16[80]{0:T(256)(128)(2,1)S(1)}, bf16[1280]{0:T(1024)(128)(2,1)S(1)}, bf16[1280]{0:T(1024)(128)(2,1)S(1)}, bf16[80]{0:T(256)(128)(2,1)S(1)}, bf16[1280]{0:T(1024)(128)(2,1)S(1)}) all-reduce(bf16[80]{0:T(256)(128)(2,1)S(1)} %dynamic-update-slice, ...), channel_id=4, replica_groups=mesh['replica'=2,'fsdp'=8,'seq'=2] {'fsdp'}, use_global_device_ids=true, to_apply=%add | all-reduce | flops 4000 | bytes 16000
  179.8 21.0 %fusion.137 = (f32[1280]{0:T(1024)S(1)}, f32[1280]{0:T(1024)S(1)}) fusion(bf16[1,2,1280]{1,0,2:T(2,128)(2,1)S(1)} %all-gather.8), kind=kLoop, calls=%fused_computation.145 | loop fusion | flops 2560 | bytes 15360 | tf_op jit(solution)/shard_map/mul | solution.py:38
  243.2 35.7 %all-gather.37.cloned.1.call-done = bf16[1,1280,1280]{2,1,0:T(8,128)(2,1)} async-done(((bf16[1,160,1280]{2,1,0:T(8,128)(2,1)}), bf16[1,1280,1280]{2,1,0:T(8,128)(2,1)}) %all-gather.37.cloned.1.call-update) | async-done | bytes 3276816 | tf_op jit(solution)/shard_map/all_gather | solution.py:261
  282.9 90.4 %all-gather.39.cloned.1.call-done = bf16[1,1280,3840]{2,1,0:T(8,128)(2,1)} async-done(((bf16[1,160,3840]{2,1,0:T(8,128)(2,1)}), bf16[1,1280,3840]{2,1,0:T(8,128)(2,1)}) %all-gather.39.cloned.1.call-update) | async-done | bytes 9830416 | tf_op jit(solution)/shard_map/all_gather | solution.py:258
  389.5 31.1 %all-gather.29.cloned.1.call-done = bf16[1,2560,512]{1,2,0:T(8,128)(2,1)} async-done(((bf16[1,2560,256]{1,2,0:T(8,128)(2,1)}), bf16[1,2560,512]{1,2,0:T(8,128)(2,1)}) %all-gather.29.cloned.1.call-update) | async-done | bytes 2621456 | tf_op jit(solution)/shard_map/all_gather | solution.py:68
  439.0 22.6 %all-gather.41.cloned.1.call-done = bf16[1,1280,1280]{2,1,0:T(8,128)(2,1)} async-done(((bf16[1,160,1280]{2,1,0:T(8,128)(2,1)}), bf16[1,1280,1280]{2,1,0:T(8,128)(2,1)}) %all-gather.41.cloned.1.call-update) | async-done | bytes 3276816 | tf_op jit(solution)/shard_map/all_gather | solution.py:259
  466.3 35.2 %all-gather.43.cloned.1.call-done = bf16[1,1280,1280]{2,1,0:T(8,128)(2,1)} async-done(((bf16[1,160,1280]{2,1,0:T(8,128)(2,1)}), bf16[1,1280,1280]{2,1,0:T(8,128)(2,1)}) %all-gather.43.cloned.1.call-update) | async-done | bytes 3276816 | tf_op jit(solution)/shard_map/all_gather | solution.py:260
  506.1 35.2 %all-gather.45.cloned.1.call-done = bf16[1,1280,1280]{2,1,0:T(8,128)(2,1)} async-done(((bf16[1,160,1280]{2,1,0:T(8,128)(2,1)}), bf16[1,1280,1280]{2,1,0:T(8,128)(2,1)}) %all-gather.45.cloned.1.call-update) | async-done | bytes 3276816 | tf_op jit(solution)/shard_map/all_gather | solution.py:261
  598.7 37.6 %reduce-scatter.19.cloned.1.call-done = f32[1,1280,256]{2,1,0:T(8,128)} async-done(((f32[1,1280,512]{2,1,0:T(8,128)}), f32[1,1280,256]{2,1,0:T(8,128)}) %reduce-scatter.19.cloned.1.call-update) | async-done | bytes 1310736 | tf_op jit(solution)/shard_map/reduce_scatter | solution.py:181
  722.4 20.2 %reduce-scatter.23.cloned.1.call-done = f32[1,1280,256]{2,1,0:T(8,128)} async-done(((f32[1,1280,512]{2,1,0:T(8,128)}), f32[1,1280,256]{2,1,0:T(8,128)}) %reduce-scatter.23.cloned.1.call-update) | async-done | bytes 1310736 | tf_op jit(solution)/shard_map/reduce_scatter | solution.py:181
  760.5 25.6 %reduce-scatter.37.cloned.1.call-done = bf16[160,1280]{1,0:T(8,128)(2,1)} async-done(((bf16[1280,1280]{1,0:T(8,128)(2,1)}), bf16[160,1280]{1,0:T(8,128)(2,1)}) %reduce-scatter.37.cloned.1.call-update) | async-done | bytes 409616 | tf_op jit(solution)/shard_map/reduce_scatter | solution.py:302
  786.1 42.4 %reduce-scatter.33.cloned.1.call-done = bf16[160,1280]{1,0:T(8,128)(2,1)} async-done(((bf16[1280,1280]{1,0:T(8,128)(2,1)}), bf16[160,1280]{1,0:T(8,128)(2,1)}) %reduce-scatter.33.cloned.1.call-update) | async-done | bytes 409616 | tf_op jit(solution)/shard_map/reduce_scatter | solution.py:299
  828.6 42.4 %reduce-scatter.41.cloned.1.call-done = bf16[160,1280]{1,0:T(8,128)(2,1)} async-done(((bf16[1280,1280]{1,0:T(8,128)(2,1)}), bf16[160,1280]{1,0:T(8,128)(2,1)}) %reduce-scatter.41.cloned.1.call-update) | async-done | bytes 409616 | tf_op jit(solution)/shard_map/reduce_scatter | solution.py:305
  870.9 42.4 %reduce-scatter.39.cloned.1.call-done = bf16[160,1280]{1,0:T(8,128)(2,1)} async-done(((bf16[1280,1280]{1,0:T(8,128)(2,1)}), bf16[160,1280]{1,0:T(8,128)(2,1)}) %reduce-scatter.39.cloned.1.call-update) | async-done | bytes 409616 | tf_op jit(solution)/shard_map/reduce_scatter | solution.py:305
  913.4 42.5 %reduce-scatter.35.cloned.1.call-done = bf16[160,1280]{1,0:T(8,128)(2,1)} async-done(((bf16[1280,1280]{1,0:T(8,128)(2,1)}), bf16[160,1280]{1,0:T(8,128)(2,1)}) %reduce-scatter.35.cloned.1.call-update) | async-done | bytes 409616 | tf_op jit(solution)/shard_map/reduce_scatter | solution.py:302
  955.9 42.4 %reduce-scatter.31.cloned.1.call-done = bf16[160,1280]{1,0:T(8,128)(2,1)} async-done(((bf16[1280,1280]{1,0:T(8,128)(2,1)}), bf16[160,1280]{1,0:T(8,128)(2,1)}) %reduce-scatter.31.cloned.1.call-update) | async-done | bytes 409616 | tf_op jit(solution)/shard_map/reduce_scatter | solution.py:299
  998.3 104.4 %reduce-scatter.29.cloned.1.call-done = bf16[160,3840]{1,0:T(8,128)(2,1)} async-done(((bf16[1280,3840]{1,0:T(8,128)(2,1)}), bf16[160,3840]{1,0:T(8,128)(2,1)}) %reduce-scatter.29.cloned.1.call-update) | async-done | bytes 1228816 | tf_op jit(solution)/shard_map/reduce_scatter | solution.py:296
  1102.7 104.0 %reduce-scatter.27.cloned.1.call-done = bf16[160,3840]{1,0:T(8,128)(2,1)} async-done(((bf16[1280,3840]{1,0:T(8,128)(2,1)}), bf16[160,3840]{1,0:T(8,128)(2,1)}) %reduce-scatter.27.cloned.1.call-update) | async-done | bytes 1228816 | tf_op jit(solution)/shard_map/reduce_scatter | solution.py:296
  1208.5 26.4 %all-reduce.12 = (bf16[1280]{0:T(1024)(128)(2,1)S(1)}, bf16[1280]{0:T(1024)(128)(2,1)S(1)}, bf16[1280]{0:T(1024)(128)(2,1)S(1)}, bf16[1280]{0:T(1024)(128)(2,1)S...) all-reduce(bf16[1280]{0:T(1024)(128)(2,1)S(1)} %dynamic-update-slic, ...), channel_id=17, replica_groups=mesh['replica'=2,'fsdp'=8,'seq'=2] {'fsdp'}, use_global_device_ids=true, to_apply=%add.5 | all-reduce | flops 6560 | bytes 26240
  1243.3 26.8 %reduce-scatter.43.cloned.1.call-done = bf16[160,2]{1,0:T(8,128)(2,1)} async-done(((bf16[1280,2]{1,0:T(8,128)(2,1)}), bf16[160,2]{1,0:T(8,128)(2,1)}) %reduce-scatter.43.cloned.1.call-update) | async-done | bytes 656
  1283.2 107.7 %all-reduce.18.cloned.1.call-done = (bf16[1,160,3840]{2,1,0:T(8,128)(2,1)}, bf16[1,160,3840]{2,1,0:T(8,128)(2,1)}, bf16[1,160,1280]{2,1,0:T(8,128)(2,1)}, bf16[1...) async-done(((bf16[1,160,3840]{2,1,0:T(8,128)(2,1)}, ...) | async-done | bytes 4915216 | tf_op jit(solution)/shard_map/psum | solution.py:322
  (319 shorter events, 325.7 us)
Async XLA Ops:
  7.2 100.7 %all-gather.31.cloned.1.call-start = ((), (), s32[]{:S(2)}) async-start(), calls=%async_computation.28 | async-start | bytes 11059200 | tf_op jit(solution)/shard_map/all_gather | solution.py:258
  10.5 192.0 %all-gather.27.cloned.1.call-start = ((), (), s32[]{:S(2)}) async-start(), calls=%async_computation.14 | async-start | bytes 3932160 | tf_op jit(solution)/shard_map/all_gather | solution.py:68
  117.7 113.2 %all-gather.33.cloned.1.call-start = ((), (), s32[]{:S(2)}) async-start(), calls=%async_computation.29 | async-start | bytes 3686400 | tf_op jit(solution)/shard_map/all_gather | solution.py:259
  119.8 119.4 %all-gather.35.cloned.1.call-start = ((), (), s32[]{:S(2)}) async-start(), calls=%async_computation.30 | async-start | bytes 3686400 | tf_op jit(solution)/shard_map/all_gather | solution.py:260
  120.8 158.1 %all-gather.37.cloned.1.call-start = ((), (), s32[]{:S(2)}) async-start(), calls=%async_computation.31 | async-start | bytes 3686400 | tf_op jit(solution)/shard_map/all_gather | solution.py:261
  122.1 251.2 %all-gather.39.cloned.1.call-start = ((), (), s32[]{:S(2)}) async-start(), calls=%async_computation.32 | async-start | bytes 11059200 | tf_op jit(solution)/shard_map/all_gather | solution.py:258
  122.6 297.9 %all-gather.29.cloned.1.call-start = ((), (), s32[]{:S(2)}) async-start(), calls=%async_computation.15 | async-start | bytes 3932160 | tf_op jit(solution)/shard_map/all_gather | solution.py:68
  383.0 78.6 %all-gather.41.cloned.1.call-start = ((), (), s32[]{:S(2)}) async-start(), calls=%async_computation.33 | async-start | bytes 3686400 | tf_op jit(solution)/shard_map/all_gather | solution.py:259
  383.7 117.8 %all-gather.43.cloned.1.call-start = ((), (), s32[]{:S(2)}) async-start(), calls=%async_computation.34 | async-start | bytes 3686400 | tf_op jit(solution)/shard_map/all_gather | solution.py:260
  384.5 156.8 %all-gather.45.cloned.1.call-start = ((), (), s32[]{:S(2)}) async-start(), calls=%async_computation.35 | async-start | bytes 3686400 | tf_op jit(solution)/shard_map/all_gather | solution.py:261
  385.1 211.4 %reduce-scatter.21.cloned.1.call-start = ((), (), s32[]{:S(2)}) async-start(), calls=%async_computation.17 | async-start | bytes 3932160 | tf_op jit(solution)/shard_map/reduce_scatter | solution.py:187
  575.0 145.9 %reduce-scatter.25.cloned.1.call-start = ((), (), s32[]{:S(2)}) async-start(), calls=%async_computation.19 | async-start | bytes 3932160 | tf_op jit(solution)/shard_map/reduce_scatter | solution.py:187
  665.1 77.5 %reduce-scatter.23.cloned.1.call-start = ((), (), s32[]{:S(2)}) async-start(), calls=%async_computation.18 | async-start | bytes 3932160 | tf_op jit(solution)/shard_map/reduce_scatter | solution.py:181
  679.9 106.2 %reduce-scatter.37.cloned.1.call-start = ((), (), s32[]{:S(2)}) async-start(), calls=%async_computation.25 | async-start | bytes 3686400 | tf_op jit(solution)/shard_map/reduce_scatter | solution.py:302
  684.3 144.3 %reduce-scatter.33.cloned.1.call-start = ((), (), s32[]{:S(2)}) async-start(), calls=%async_computation.23 | async-start | bytes 3686400 | tf_op jit(solution)/shard_map/reduce_scatter | solution.py:299
  688.6 182.4 %reduce-scatter.41.cloned.1.call-start = ((), (), s32[]{:S(2)}) async-start(), calls=%async_computation.27 | async-start | bytes 3686400 | tf_op jit(solution)/shard_map/reduce_scatter | solution.py:305
  693.1 220.2 %reduce-scatter.39.cloned.1.call-start = ((), (), s32[]{:S(2)}) async-start(), calls=%async_computation.26 | async-start | bytes 3686400 | tf_op jit(solution)/shard_map/reduce_scatter | solution.py:305
  698.0 257.9 %reduce-scatter.35.cloned.1.call-start = ((), (), s32[]{:S(2)}) async-start(), calls=%async_computation.24 | async-start | bytes 3686400 | tf_op jit(solution)/shard_map/reduce_scatter | solution.py:302
  702.3 296.0 %reduce-scatter.31.cloned.1.call-start = ((), (), s32[]{:S(2)}) async-start(), calls=%async_computation.22 | async-start | bytes 3686400 | tf_op jit(solution)/shard_map/reduce_scatter | solution.py:299
  706.7 396.0 %reduce-scatter.29.cloned.1.call-start = ((), (), s32[]{:S(2)}) async-start(), calls=%async_computation.21 | async-start | bytes 11059200 | tf_op jit(solution)/shard_map/reduce_scatter | solution.py:296
  715.1 491.7 %reduce-scatter.27.cloned.1.call-start = ((), (), s32[]{:S(2)}) async-start(), calls=%async_computation.20 | async-start | bytes 11059200 | tf_op jit(solution)/shard_map/reduce_scatter | solution.py:296
  750.7 489.2 %reduce-scatter.45.cloned.1.call-start = ((), (), s32[]{:S(2)}) async-start(), calls=%async_computation.37 | async-start | bytes 368640
  751.7 518.3 %reduce-scatter.43.cloned.1.call-start = ((), (), s32[]{:S(2)}) async-start(), calls=%async_computation.36 | async-start | bytes 368640
  760.5 630.4 %all-reduce.18.cloned.1.call-start = ((), (), s32[]{:S(2)}) async-start(), calls=%async_computation.38 | async-start | bytes 9830400 | tf_op jit(solution)/shard_map/psum | solution.py:322
  (62 other events, 678.4 us)
Sparse Core Ops, SparseCore 0:
  10.6 97.2 all-gather.30
  117.8 37.5 all-gather.26
  157.6 40.0 all-gather.32
  199.8 39.3 all-gather.34
  240.6 38.2 all-gather.36
  280.4 92.8 all-gather.38
  383.1 37.4 all-gather.28
  422.2 39.3 all-gather.40
  463.3 38.2 all-gather.42
  503.0 38.2 all-gather.44
  560.0 36.4 reduce-scatter.20
  598.6 37.5 reduce-scatter.18
  665.2 37.5 reduce-scatter.24
  704.9 37.5 reduce-scatter.22
  744.7 41.3 reduce-scatter.36
  788.4 40.1 reduce-scatter.32
  830.7 40.1 reduce-scatter.40
  873.2 40.1 reduce-scatter.38
  915.7 40.1 reduce-scatter.34
  958.1 40.1 reduce-scatter.30
  1000.6 102.0 reduce-scatter.28
  1105.1 101.5 reduce-scatter.26
  1209.6 28.8 reduce-scatter.44
  1274.5 116.3 all-reduce.17
  (1 shorter events, 28.6 us)
where the time goes:
time: 1420 us; the launch traced here: 1410 us
  waiting for transfers between devices  971 us (68%)
  matrix products  173 us (12%)
  blocking collectives  96.6 us (7%)
  other arithmetic  82.8 us (6%)
  local copies, waits for them, and re-layouts  59.5 us (4%)
  between operations  21.9 us (2%)
    reduce_scatter x2, waiting for transfers between devices, shards(): lax.psum_scatter(layer_grads[0].astype(jnp.bfloat16), 'fsdp', scatter_dim...  208 us
    all_gather x2, waiting for transfers between devices, shards(): lax.all_gather(qkv_weight[layer_index], 'fsdp', axis=0, tiled=True)  148 us
    psum x1, waiting for transfers between devices, shards(): lax.psum(shares[0].astype(jnp.bfloat16), ('replica', 'seq'))  108 us
    reduce_scatter x2, waiting for transfers between devices, shards(): lax.psum_scatter(layer_grads[1].astype(jnp.bfloat16), 'fsdp', scatter_dim...  84.9 us
    reduce_scatter x2, waiting for transfers between devices, shards(): lax.psum_scatter(layer_grads[3].astype(jnp.bfloat16), 'fsdp', scatter_dim...  84.8 us
    all_gather x2, waiting for transfers between devices, shards(): lax.all_gather(down_weight[layer_index], 'fsdp', axis=0, tiled=True)  70.9 us
    reduce_scatter x2, waiting for transfers between devices, shards(): lax.psum_scatter(layer_grads[2].astype(jnp.bfloat16), 'fsdp', scatter_dim...  68.1 us
    reduce_scatter x2, waiting for transfers between devices, backward_layer(): lax.psum_scatter(key_grad.reshape(series_count, model_width, total_length...  57.8 us
  transfers between devices with their start and end apart: 25, of which 21 were waited for; matrix products, arithmetic and copies ran while one was open for 16% of the time, Pallas kernels for 0%

commit v1 on v0

--- a/solution.py
+++ b/solution.py
@@ -318,8 +318,14 @@
                 layer_grads[7].astype(jnp.bfloat16), "fsdp", scatter_dimension=0, tiled=True
             ).astype(jnp.float32),
         )
+
+        def _put_screen(w_in):
+            for pp in ("seq", "replica"):
+                w_in = jax.lax.psum(w_in, pp)
+            return w_in
+
         shares = (
-            lax.psum(shares[0].astype(jnp.bfloat16), ("replica", "seq")).astype(jnp.float32),
+            _put_screen(shares[0].astype(jnp.bfloat16)).astype(jnp.float32),
             lax.psum(shares[1].astype(jnp.bfloat16), ("replica", "seq")).astype(jnp.float32),
             lax.psum(shares[2].astype(jnp.bfloat16), ("replica", "seq")).astype(jnp.float32),
             lax.psum(shares[3].astype(jnp.bfloat16), ("replica", "seq")).astype(jnp.float32),

time: 1420 us -> 1520 us (1.070)
  waiting for transfers between devices: 971 us -> 1060 us
    psum x1 -> x3, waiting for transfers between devices: 108 us -> 175 us  [the longest x2 110 us: _put_screen(): w_in = jax.lax.psum(w_in, pp)]
    reduce_scatter x2, waiting for transfers between devices: 208 us -> 170 us  [shards(): lax.psum_scatter(layer_grads[0].astype(jnp.bfloat16), 'fsdp', scatter_dim...]
    unnamed x27 -> x29, waiting for transfers between devices: 29.5 us -> 59.4 us
    reduce_scatter x2, waiting for transfers between devices: 57.8 us -> 76 us  [backward_layer(): lax.psum_scatter(key_grad.reshape(series_count, model_width, total_length...]
  transfers between devices with their start and end apart: 25 -> 27, of which waited for: 21 -> 25; matrix products, arithmetic and copies ran while one was open for 16% -> 16% of each run, Pallas kernels for 0% -> 0%
where the time goes in v1:
time: 1520 us; the launch traced here: 1510 us
  waiting for transfers between devices  1060 us (70%)
  matrix products  170 us (11%)
  blocking collectives  97.7 us (6%)
  other arithmetic  87.3 us (6%)
  local copies, waits for them, and re-layouts  66.3 us (4%)
  between operations  22.2 us (1%)
    reduce_scatter x2, waiting for transfers between devices, shards(): lax.psum_scatter(layer_grads[0].astype(jnp.bfloat16), 'fsdp', scatter_dim...  170 us
    all_gather x2, waiting for transfers between devices, shards(): lax.all_gather(qkv_weight[layer_index], 'fsdp', axis=0, tiled=True)  148 us
    psum x2, waiting for transfers between devices, _put_screen(): w_in = jax.lax.psum(w_in, pp)  110 us
    reduce_scatter x2, waiting for transfers between devices, shards(): lax.psum_scatter(layer_grads[1].astype(jnp.bfloat16), 'fsdp', scatter_dim...  85.7 us
    reduce_scatter x2, waiting for transfers between devices, shards(): lax.psum_scatter(layer_grads[3].astype(jnp.bfloat16), 'fsdp', scatter_dim...  85 us
    reduce_scatter x2, waiting for transfers between devices, backward_layer(): lax.psum_scatter(key_grad.reshape(series_count, model_width, total_length...  76 us
    reduce_scatter x2, waiting for transfers between devices, shards(): lax.psum_scatter(layer_grads[2].astype(jnp.bfloat16), 'fsdp', scatter_dim...  73.9 us
    all_gather x2, waiting for transfers between devices, shards(): lax.all_gather(down_weight[layer_index], 'fsdp', axis=0, tiled=True)  71 us
  transfers between devices with their start and end apart: 27, of which 25 were waited for; matrix products, arithmetic and copies ran while one was open for 16% of the time, Pallas kernels for 0%

profile of v1, /device:TPU:0, one launch (start us, length us, event | category | flops | bytes accessed | tf_op | source)
XLA Modules:
  0.0 1507.5 jit_solution(12112051656863880916)
XLA Ops:
  49.9 58.0 %all-gather.31.cloned.1.call-done = bf16[1,1280,3840]{2,1,0:T(8,128)(2,1)} async-done(((bf16[1,160,3840]{2,1,0:T(8,128)(2,1)}), bf16[1,1280,3840]{2,1,0:T(8,128)(2,1)}) %all-gather.31.cloned.1.call-update) | async-done | bytes 9830416 | tf_op jit(solution)/shard_map/all_gather | solution.py:258
  131.1 26.5 %all-reduce.13 = (bf16[80]{0:T(256)(128)(2,1)S(1)}, bf16[1280]{0:T(1024)(128)(2,1)S(1)}, bf16[1280]{0:T(1024)(128)(2,1)S(1)}, bf16[80]{0:T(256)(128)(2,1)S(1)}, bf16[1280]{0:T(1024)(128)(2,1)S(1)}) all-reduce(bf16[80]{0:T(256)(128)(2,1)S(1)} %dynamic-update-slice, ...), channel_id=4, replica_groups=mesh['replica'=2,'fsdp'=8,'seq'=2] {'fsdp'}, use_global_device_ids=true, to_apply=%add | all-reduce | flops 4000 | bytes 16000
  243.2 35.7 %all-gather.37.cloned.1.call-done = bf16[1,1280,1280]{2,1,0:T(8,128)(2,1)} async-done(((bf16[1,160,1280]{2,1,0:T(8,128)(2,1)}), bf16[1,1280,1280]{2,1,0:T(8,128)(2,1)}) %all-gather.37.cloned.1.call-update) | async-done | bytes 3276816 | tf_op jit(solution)/shard_map/all_gather | solution.py:261
  283.5 89.8 %all-gather.39.cloned.1.call-done = bf16[1,1280,3840]{2,1,0:T(8,128)(2,1)} async-done(((bf16[1,160,3840]{2,1,0:T(8,128)(2,1)}), bf16[1,1280,3840]{2,1,0:T(8,128)(2,1)}) %all-gather.39.cloned.1.call-update) | async-done | bytes 9830416 | tf_op jit(solution)/shard_map/all_gather | solution.py:258
  389.4 31.1 %all-gather.29.cloned.1.call-done = bf16[1,2560,512]{1,2,0:T(8,128)(2,1)} async-done(((bf16[1,2560,256]{1,2,0:T(8,128)(2,1)}), bf16[1,2560,512]{1,2,0:T(8,128)(2,1)}) %all-gather.29.cloned.1.call-update) | async-done | bytes 2621456 | tf_op jit(solution)/shard_map/all_gather | solution.py:68
  439.0 22.6 %all-gather.41.cloned.1.call-done = bf16[1,1280,1280]{2,1,0:T(8,128)(2,1)} async-done(((bf16[1,160,1280]{2,1,0:T(8,128)(2,1)}), bf16[1,1280,1280]{2,1,0:T(8,128)(2,1)}) %all-gather.41.cloned.1.call-update) | async-done | bytes 3276816 | tf_op jit(solution)/shard_map/all_gather | solution.py:259
  466.8 34.7 %all-gather.43.cloned.1.call-done = bf16[1,1280,1280]{2,1,0:T(8,128)(2,1)} async-done(((bf16[1,160,1280]{2,1,0:T(8,128)(2,1)}), bf16[1,1280,1280]{2,1,0:T(8,128)(2,1)}) %all-gather.43.cloned.1.call-update) | async-done | bytes 3276816 | tf_op jit(solution)/shard_map/all_gather | solution.py:260
  506.0 35.3 %all-gather.45.cloned.1.call-done = bf16[1,1280,1280]{2,1,0:T(8,128)(2,1)} async-done(((bf16[1,160,1280]{2,1,0:T(8,128)(2,1)}), bf16[1,1280,1280]{2,1,0:T(8,128)(2,1)}) %all-gather.45.cloned.1.call-update) | async-done | bytes 3276816 | tf_op jit(solution)/shard_map/all_gather | solution.py:261
  598.6 37.6 %reduce-scatter.19.cloned.1.call-done = f32[1,1280,256]{2,1,0:T(8,128)} async-done(((f32[1,1280,512]{2,1,0:T(8,128)}), f32[1,1280,256]{2,1,0:T(8,128)}) %reduce-scatter.19.cloned.1.call-update) | async-done | bytes 1310736 | tf_op jit(solution)/shard_map/reduce_scatter | solution.py:181
  704.2 38.4 %reduce-scatter.23.cloned.1.call-done = f32[1,1280,256]{2,1,0:T(8,128)} async-done(((f32[1,1280,512]{2,1,0:T(8,128)}), f32[1,1280,256]{2,1,0:T(8,128)}) %reduce-scatter.23.cloned.1.call-update) | async-done | bytes 1310736 | tf_op jit(solution)/shard_map/reduce_scatter | solution.py:181
  782.2 65.9 %reduce-scatter.29.cloned.1.call-done = bf16[160,3840]{1,0:T(8,128)(2,1)} async-done(((bf16[1280,3840]{1,0:T(8,128)(2,1)}), bf16[160,3840]{1,0:T(8,128)(2,1)}) %reduce-scatter.29.cloned.1.call-update) | async-done | bytes 1228816 | tf_op jit(solution)/shard_map/reduce_scatter | solution.py:296
  848.0 103.9 %reduce-scatter.27.cloned.1.call-done = bf16[160,3840]{1,0:T(8,128)(2,1)} async-done(((bf16[1280,3840]{1,0:T(8,128)(2,1)}), bf16[160,3840]{1,0:T(8,128)(2,1)}) %reduce-scatter.27.cloned.1.call-update) | async-done | bytes 1228816 | tf_op jit(solution)/shard_map/reduce_scatter | solution.py:296
  962.4 31.4 %reduce-scatter.37.cloned.1.call-done = bf16[160,1280]{1,0:T(8,128)(2,1)} async-done(((bf16[1280,1280]{1,0:T(8,128)(2,1)}), bf16[160,1280]{1,0:T(8,128)(2,1)}) %reduce-scatter.37.cloned.1.call-update) | async-done | bytes 409616 | tf_op jit(solution)/shard_map/reduce_scatter | solution.py:302
  993.8 43.0 %reduce-scatter.33.cloned.1.call-done = bf16[160,1280]{1,0:T(8,128)(2,1)} async-done(((bf16[1280,1280]{1,0:T(8,128)(2,1)}), bf16[160,1280]{1,0:T(8,128)(2,1)}) %reduce-scatter.33.cloned.1.call-update) | async-done | bytes 409616 | tf_op jit(solution)/shard_map/reduce_scatter | solution.py:299
  1036.9 42.5 %reduce-scatter.41.cloned.1.call-done = bf16[160,1280]{1,0:T(8,128)(2,1)} async-done(((bf16[1280,1280]{1,0:T(8,128)(2,1)}), bf16[160,1280]{1,0:T(8,128)(2,1)}) %reduce-scatter.41.cloned.1.call-update) | async-done | bytes 409616 | tf_op jit(solution)/shard_map/reduce_scatter | solution.py:305
  1079.4 42.5 %reduce-scatter.39.cloned.1.call-done = bf16[160,1280]{1,0:T(8,128)(2,1)} async-done(((bf16[1280,1280]{1,0:T(8,128)(2,1)}), bf16[160,1280]{1,0:T(8,128)(2,1)}) %reduce-scatter.39.cloned.1.call-update) | async-done | bytes 409616 | tf_op jit(solution)/shard_map/reduce_scatter | solution.py:305
  1121.8 42.5 %reduce-scatter.35.cloned.1.call-done = bf16[160,1280]{1,0:T(8,128)(2,1)} async-done(((bf16[1280,1280]{1,0:T(8,128)(2,1)}), bf16[160,1280]{1,0:T(8,128)(2,1)}) %reduce-scatter.35.cloned.1.call-update) | async-done | bytes 409616 | tf_op jit(solution)/shard_map/reduce_scatter | solution.py:302
  1164.4 42.6 %reduce-scatter.31.cloned.1.call-done = bf16[160,1280]{1,0:T(8,128)(2,1)} async-done(((bf16[1280,1280]{1,0:T(8,128)(2,1)}), bf16[160,1280]{1,0:T(8,128)(2,1)}) %reduce-scatter.31.cloned.1.call-update) | async-done | bytes 409616 | tf_op jit(solution)/shard_map/reduce_scatter | solution.py:299
  1209.8 27.4 %all-reduce.12 = (bf16[1280]{0:T(1024)(128)(2,1)S(1)}, bf16[1280]{0:T(1024)(128)(2,1)S(1)}, bf16[1280]{0:T(1024)(128)(2,1)S(1)}, bf16[1280]{0:T(1024)(128)(2,1)S...) all-reduce(bf16[1280]{0:T(1024)(128)(2,1)S(1)} %dynamic-update-slic, ...), channel_id=17, replica_groups=mesh['replica'=2,'fsdp'=8,'seq'=2] {'fsdp'}, use_global_device_ids=true, to_apply=%add.5 | all-reduce | flops 6560 | bytes 26240
  1237.2 42.0 %all-reduce.24.cloned.1.call-done = (bf16[160,3840]{1,0:T(8,128)(2,1)}, bf16[160,3840]{1,0:T(8,128)(2,1)}) async-done(((bf16[160,3840]{1,0:T(8,128)(2,1)}, bf16[160,3840]{1,0:T(8,128)(2,1)}), (bf16[160,3840]{1,0:T(8,128)(2,1)}, bf16[160,3840]{1,0:T(8,128)(2,1)})) %all-reduce.24.cloned.1.call-update) | async-done | bytes 2457616 | tf_op jit(solution)/shard_map/psum | solution.py:324
  1284.0 28.3 %reduce-scatter.45.cloned.1.call-done = bf16[160,2]{1,0:T(8,128)(2,1)} async-done(((bf16[1280,2]{1,0:T(8,128)(2,1)}), bf16[160,2]{1,0:T(8,128)(2,1)}) %reduce-scatter.45.cloned.1.call-update) | async-done | bytes 656
  1315.8 28.2 %reduce-scatter.43.cloned.1.call-done = bf16[160,2]{1,0:T(8,128)(2,1)} async-done(((bf16[1280,2]{1,0:T(8,128)(2,1)}), bf16[160,2]{1,0:T(8,128)(2,1)}) %reduce-scatter.43.cloned.1.call-update) | async-done | bytes 656
  1357.3 65.5 %all-reduce.22.cloned.1.call-done = (bf16[1,160,1280]{2,1,0:T(8,128)(2,1)}, bf16[1,160,1280]{2,1,0:T(8,128)(2,1)}, bf16[1,160,1280]{2,1,0:T(8,128)(2,1)}, bf16[1...) async-done(((bf16[1,160,1280]{2,1,0:T(8,128)(2,1)}, bf16[1,160,1280]{2,1,0:T(8,128)(2,1)}, bf16[1,160,1280]{2,1,0:T(8,128)(2,1)}, ...) | async-done | bytes 2457616 | tf_op jit(solution)/shard_map/psum | solution.py:329
  1427.9 68.1 %all-reduce.26.cloned.1.call-done = (bf16[1,160,3840]{2,1,0:T(8,128)(2,1)}, bf16[1,160,3840]{2,1,0:T(8,128)(2,1)}) async-done(((bf16[1,160,3840]{2,1,0:T(8,128)(2,1)}, bf16[1,160,3840]{2,1,0:T(8,128)(2,1)}), (bf16[1,160,3840]{2,1,0:T(8,128)(2,1)}, bf16[1,160,3840]{2,1,0:T(8,128)(2,1)})) %all-reduce.26.cloned.1.call-update) | async-done | bytes 2457616 | tf_op jit(solution)/shard_map/psum | solution.py:324
  (331 shorter events, 401.9 us)
Async XLA Ops:
  7.2 100.7 %all-gather.31.cloned.1.call-start = ((), (), s32[]{:S(2)}) async-start(), calls=%async_computation.28 | async-start | bytes 11059200 | tf_op jit(solution)/shard_map/all_gather | solution.py:258
  10.5 192.0 %all-gather.27.cloned.1.call-start = ((), (), s32[]{:S(2)}) async-start(), calls=%async_computation.14 | async-start | bytes 3932160 | tf_op jit(solution)/shard_map/all_gather | solution.py:68
  117.7 113.2 %all-gather.33.cloned.1.call-start = ((), (), s32[]{:S(2)}) async-start(), calls=%async_computation.29 | async-start | bytes 3686400 | tf_op jit(solution)/shard_map/all_gather | solution.py:259
  119.7 119.4 %all-gather.35.cloned.1.call-start = ((), (), s32[]{:S(2)}) async-start(), calls=%async_computation.30 | async-start | bytes 3686400 | tf_op jit(solution)/shard_map/all_gather | solution.py:260
  120.8 158.1 %all-gather.37.cloned.1.call-start = ((), (), s32[]{:S(2)}) async-start(), calls=%async_computation.31 | async-start | bytes 3686400 | tf_op jit(solution)/shard_map/all_gather | solution.py:261
  122.0 251.2 %all-gather.39.cloned.1.call-start = ((), (), s32[]{:S(2)}) async-start(), calls=%async_computation.32 | async-start | bytes 11059200 | tf_op jit(solution)/shard_map/all_gather | solution.py:258
  122.6 297.9 %all-gather.29.cloned.1.call-start = ((), (), s32[]{:S(2)}) async-start(), calls=%async_computation.15 | async-start | bytes 3932160 | tf_op jit(solution)/shard_map/all_gather | solution.py:68
  383.7 117.8 %all-gather.43.cloned.1.call-start = ((), (), s32[]{:S(2)}) async-start(), calls=%async_computation.34 | async-start | bytes 3686400 | tf_op jit(solution)/shard_map/all_gather | solution.py:260
  384.5 156.8 %all-gather.45.cloned.1.call-start = ((), (), s32[]{:S(2)}) async-start(), calls=%async_computation.35 | async-start | bytes 3686400 | tf_op jit(solution)/shard_map/all_gather | solution.py:261
  385.0 211.3 %reduce-scatter.21.cloned.1.call-start = ((), (), s32[]{:S(2)}) async-start(), calls=%async_computation.17 | async-start | bytes 3932160 | tf_op jit(solution)/shard_map/reduce_scatter | solution.py:187
  574.9 127.9 %reduce-scatter.25.cloned.1.call-start = ((), (), s32[]{:S(2)}) async-start(), calls=%async_computation.19 | async-start | bytes 3932160 | tf_op jit(solution)/shard_map/reduce_scatter | solution.py:187
  679.9 168.2 %reduce-scatter.29.cloned.1.call-start = ((), (), s32[]{:S(2)}) async-start(), calls=%async_computation.21 | async-start | bytes 11059200 | tf_op jit(solution)/shard_map/reduce_scatter | solution.py:296
  688.1 263.9 %reduce-scatter.27.cloned.1.call-start = ((), (), s32[]{:S(2)}) async-start(), calls=%async_computation.20 | async-start | bytes 11059200 | tf_op jit(solution)/shard_map/reduce_scatter | solution.py:296
  750.7 243.1 %reduce-scatter.37.cloned.1.call-start = ((), (), s32[]{:S(2)}) async-start(), calls=%async_computation.25 | async-start | bytes 3686400 | tf_op jit(solution)/shard_map/reduce_scatter | solution.py:302
  755.4 281.4 %reduce-scatter.33.cloned.1.call-start = ((), (), s32[]{:S(2)}) async-start(), calls=%async_computation.23 | async-start | bytes 3686400 | tf_op jit(solution)/shard_map/reduce_scatter | solution.py:299
  760.6 318.8 %reduce-scatter.41.cloned.1.call-start = ((), (), s32[]{:S(2)}) async-start(), calls=%async_computation.27 | async-start | bytes 3686400 | tf_op jit(solution)/shard_map/reduce_scatter | solution.py:305
  766.0 355.8 %reduce-scatter.39.cloned.1.call-start = ((), (), s32[]{:S(2)}) async-start(), calls=%async_computation.26 | async-start | bytes 3686400 | tf_op jit(solution)/shard_map/reduce_scatter | solution.py:305
  771.7 392.7 %reduce-scatter.35.cloned.1.call-start = ((), (), s32[]{:S(2)}) async-start(), calls=%async_computation.24 | async-start | bytes 3686400 | tf_op jit(solution)/shard_map/reduce_scatter | solution.py:302
  777.0 430.0 %reduce-scatter.31.cloned.1.call-start = ((), (), s32[]{:S(2)}) async-start(), calls=%async_computation.22 | async-start | bytes 3686400 | tf_op jit(solution)/shard_map/reduce_scatter | solution.py:299
  782.1 497.1 %all-reduce.24.cloned.1.call-start = ((), (), s32[]{:S(2)}) async-start(), calls=%async_computation.39 | async-start | bytes 4915200 | tf_op jit(solution)/shard_map/psum | solution.py:324
  952.0 360.4 %reduce-scatter.45.cloned.1.call-start = ((), (), s32[]{:S(2)}) async-start(), calls=%async_computation.37 | async-start | bytes 368640
  953.0 391.0 %reduce-scatter.43.cloned.1.call-start = ((), (), s32[]{:S(2)}) async-start(), calls=%async_computation.36 | async-start | bytes 368640
  962.4 460.4 %all-reduce.22.cloned.1.call-start = ((), (), s32[]{:S(2)}) async-start(), calls=%async_computation.38 | async-start | bytes 4915200 | tf_op jit(solution)/shard_map/psum | solution.py:329
  1207.0 289.0 %all-reduce.26.cloned.1.call-start = ((), (), s32[]{:S(2)}) async-start(), calls=%async_computation.40 | async-start | bytes 4915200 | tf_op jit(solution)/shard_map/psum | solution.py:324
  (67 other events, 725.2 us)
Sparse Core Ops, SparseCore 0:
  10.6 97.2 all-gather.30
  117.8 37.5 all-gather.26
  157.6 40.0 all-gather.32
  199.8 39.3 all-gather.34
  240.6 38.2 all-gather.36
  280.4 92.8 all-gather.38
  383.1 37.4 all-gather.28
  422.2 39.3 all-gather.40
  463.3 38.2 all-gather.42
  503.0 38.2 all-gather.44
  598.5 37.5 reduce-scatter.18
  665.1 37.5 reduce-scatter.24
  705.0 37.5 reduce-scatter.22
  744.8 103.2 reduce-scatter.28
  850.3 101.5 reduce-scatter.26
  954.1 39.6 reduce-scatter.36
  996.7 40.1 reduce-scatter.32
  1039.2 40.1 reduce-scatter.40
  1081.6 40.1 reduce-scatter.38
  1124.2 40.1 reduce-scatter.34
  1166.8 40.1 reduce-scatter.30
  1209.4 69.7 all-reduce.23
  1347.7 75.0 all-reduce.21
  1425.0 70.9 all-reduce.25
  (3 shorter events, 95.4 us)
